TPU v7x, 32 devices: a whole 2x2x4 slice. The times are simulated.
32 devices in a mesh: groups: 2 (over y), prow: 4 (over x, core), pcol: 4 (over z).
Axes of the slice: x: 2, y: 2, z: 4, core: 2. Of those that a mesh axis runs over, the one named last changes fastest.
Arguments:
- anc_inverse: float32 [4096, 2048], P(('groups', 'prow'), 'pcol'), parts along dimension 0
- anc_factor: float32 [8, 2048, 256], P('groups', ('prow', 'pcol')), parts along dimension 0, may hold values from -0.0625 to 0.0625
- win_factor: float32 [12, 256, 256], P('groups'), parts along dimension 0, may hold values from -0.1875 to 0.1875
- diag_inverse: float32 [8, 256, 256], P('groups'), parts along dimension 0
- first_reader: int32 [32], P('groups'), parts along dimension 0, may hold values from 0 to 4
Outputs:
- anc_panels: float32 [8, 2048, 256], P('groups', ('prow', 'pcol')), parts along dimension 0
- window_inverse: float32 [8, 4, 256, 256], P('groups'), parts along dimension 0
There are 2 independent parts, one for each index of `groups`. A program takes and returns all parts, laid end to end along the dimension named above; each array names one. Nothing has to cross between parts.
Inputs may be any that keep to these rules, and one draw needn't show every extreme that they name: Ancestor block b belongs to the pattern of supernode k exactly when first_reader[b] <= k; the value 4 puts it in no pattern, so patterns grow with k. Within each part, anc_inverse is symmetric: anc_inverse[r, s] = anc_inverse[s, r].
All inputs are finite; a program needn't handle non-finite values.
Results may differ from a plain program's by a relative error of at most 0.0003.
Values sent between devices are 32-bit elements; how exact they have to be, the bound alone decides.
A program may use at most 64 MiB of HBM per device.

v0:
```python
import jax
import jax.numpy as jnp
from jax import lax
from jax.sharding import PartitionSpec as P

BLK = 128


def broadcast(array, axis, root):
    mine = lax.axis_index(axis) == root
    return lax.psum(jnp.where(mine, array, jnp.zeros_like(array)), axis)


def to_columns(stacked, per_column, pcol_at):
    gathered = lax.all_gather(stacked, "pcol", axis=1, tiled=True)
    pieces = [
        broadcast(gathered, "prow", pcol_at * per_column + offset) for offset in range(per_column)
    ]
    return jnp.concatenate(pieces, axis=1)


def window_algebra(summed, upper_all, diag_inverse, window_count):
    highest = lax.Precision.HIGHEST
    blocks = [[None] * window_count for column in range(window_count)]
    for node in reversed(range(window_count)):
        linv = diag_inverse[node]
        later = list(range(node + 1, window_count))
        upper_u = upper_all[node]
        cross = {}
        for position, other in enumerate(later):
            term = summed[node][position]
            for second in later:
                term = term + jnp.dot(blocks[other][second], upper_u[second], precision=highest)
            cross[other] = term
        own = jnp.dot(linv.T, linv, precision=highest) + summed[node][len(later)]
        for other in later:
            own = own + jnp.dot(upper_u[other].T, cross[other], precision=highest)
        blocks[node][node] = own
        for other in later:
            blocks[other][node] = -cross[other]
            blocks[node][other] = -cross[other].T
    return jnp.stack([jnp.stack(blocks[row_at]) for row_at in range(window_count)])


def per_device(anc_inverse, anc_factor, win_factor, diag_inverse, first_reader):
    highest = lax.Precision.HIGHEST
    n_prow = lax.axis_size("prow")
    n_pcol = lax.axis_size("pcol")
    per_column = n_prow // n_pcol
    prow_at = lax.axis_index("prow")
    pcol_at = lax.axis_index("pcol")
    window_count = diag_inverse.shape[0]
    fine_rows = anc_factor.shape[1]
    start_row = (prow_at * n_pcol + pcol_at) * fine_rows
    block_of = (start_row + jnp.arange(fine_rows, dtype=jnp.int32)) // BLK
    block_ids = jnp.arange(first_reader.shape[0], dtype=jnp.int32)
    readers = jnp.sum(
        jnp.where(block_of[:, None] == block_ids[None, :], first_reader[None, :], 0), axis=1
    )
    row_masks = [(readers <= node).astype(jnp.float32)[:, None] for node in range(window_count)]
    lower_all = [
        jnp.dot(anc_factor[node], diag_inverse[node], precision=highest) * row_masks[node]
        for node in range(window_count)
    ]
    whole = to_columns(jnp.stack(lower_all), per_column, pcol_at)
    column_panels = [whole[node] for node in range(window_count)]
    panels = [None] * window_count
    upper_all = [None] * window_count
    summed = [None] * window_count
    for node in reversed(range(window_count)):
        linv = diag_inverse[node]
        later = list(range(node + 1, window_count))
        upper_u = {}
        for other in later:
            upper_u[other] = jnp.dot(
                win_factor[other * (other - 1) // 2 + node], linv, precision=highest
            )
        upper_all[node] = upper_u
        columns = column_panels[node]
        full_x = lax.psum_scatter(
            jnp.dot(anc_inverse, columns, precision=highest),
            "pcol",
            scatter_dimension=0,
            tiled=True,
        )
        for other in later:
            full_x = full_x + jnp.dot(panels[other], upper_u[other], precision=highest)
        partials = [jnp.dot(panels[other].T, lower_all[node], precision=highest) for other in later]
        partials.append(jnp.dot(lower_all[node].T, full_x, precision=highest))
        panels[node] = -full_x * row_masks[node]
        summed[node] = list(lax.psum(tuple(partials), ("prow", "pcol")))
    window_inverse = window_algebra(summed, upper_all, diag_inverse, window_count)
    return (jnp.stack(panels), window_inverse)


def solution(mesh):
    return jax.shard_map(
        per_device,
        mesh=mesh,
        in_specs=(
            P(("groups", "prow"), "pcol"),
            P("groups", ("prow", "pcol"), None),
            P("groups", None, None),
            P("groups", None, None),
            P("groups"),
        ),
        out_specs=(P("groups", ("prow", "pcol"), None), P("groups", None, None, None)),
        check_vma=False,
    )
```

profile of v0, /device:TPU:0, one launch (start us, length us, event | category | flops | bytes accessed | tf_op | source)
XLA Modules:
  0.0 358.3 jit_solution(12927005311065160913)
XLA Ops:
  8.1 1.3 convolution_multiply_fusion.3
  9.4 1.3 convolution_multiply_fusion.2
  10.8 1.3 convolution_multiply_fusion.1
  12.1 1.3 convolution_multiply_fusion
  14.4 48.7 %all-gather.2.cloned.1.call-done = f32[4,512,256]{2,1,0:T(8,128)} async-done(((f32[4,128,256]{2,1,0:T(8,128)}), f32[4,512,256]{2,1,0:T(8,128)}) %all-gather.2.cloned.1.call-update) | async-done | bytes 2097168 | tf_op jit(solution)/shard_map/all_gather | solution.py:15
  63.2 3.1 broadcast_select_fusion
  66.3 50.1 %all-reduce.4.cloned.1.call-done = f32[4,512,256]{2,1,0:T(8,128)} async-done(((f32[4,512,256]{2,1,0:T(8,128)}), f32[4,512,256]{2,1,0:T(8,128)}) %all-reduce.4.cloned.1.call-update) | async-done | bytes 2097168 | tf_op jit(solution)/shard_map/psum | solution.py:11
  116.4 2.8 convolution_bitcast_fusion
  119.4 2.9 convolution_bitcast_fusion.1
  122.4 1.3 fusion.5
  123.7 1.3 fusion.1
  125.0 2.9 convolution_bitcast_fusion.2
  128.0 1.3 fusion.3
  129.3 1.3 fusion.7
  130.7 1.3 fusion.9
  132.0 2.1 fusion.11
  134.1 2.9 convolution_bitcast_fusion.3
  137.2 4.0 %reduce-scatter.11.cloned.1.call-done = f32[128,256]{1,0:T(8,128)} async-done(((f32[512,256]{1,0:T(8,128)}), f32[128,256]{1,0:T(8,128)}) %reduce-scatter.11.cloned.1.call-update) | async-done | bytes 131088 | tf_op jit(solution)/shard_map/reduce_scatter | solution.py:80
  141.2 22.7 %reduce-scatter.9.cloned.1.call-done = f32[128,256]{1,0:T(8,128)} async-done(((f32[512,256]{1,0:T(8,128)}), f32[128,256]{1,0:T(8,128)}) %reduce-scatter.9.cloned.1.call-update) | async-done | bytes 131088 | tf_op jit(solution)/shard_map/reduce_scatter | solution.py:80
  163.9 1.4 convolution_add_fusion.29
  165.3 20.7 %reduce-scatter.7.cloned.1.call-done = f32[128,256]{1,0:T(8,128)} async-done(((f32[512,256]{1,0:T(8,128)}), f32[128,256]{1,0:T(8,128)}) %reduce-scatter.7.cloned.1.call-update) | async-done | bytes 131088 | tf_op jit(solution)/shard_map/reduce_scatter | solution.py:80
  186.0 1.3 convolution_add_fusion.28
  187.3 1.2 convolution_add_fusion.27
  188.5 2.2 fusion.80
  190.7 2.0 fusion.79
  192.7 2.1 fusion.66
  194.8 2.1 fusion.65
  196.8 1.2 fusion.63
  198.0 10.0 %reduce-scatter.5.cloned.1.call-done = f32[128,256]{1,0:T(8,128)} async-done(((f32[512,256]{1,0:T(8,128)}), f32[128,256]{1,0:T(8,128)}) %reduce-scatter.5.cloned.1.call-update) | async-done | bytes 131088 | tf_op jit(solution)/shard_map/reduce_scatter | solution.py:80
  208.1 1.3 convolution_add_fusion.26
  209.4 1.2 convolution_add_fusion.25
  211.0 2.1 fusion.78
  213.1 1.1 fusion.81
  214.2 1.2 fusion.76
  215.4 1.2 fusion.75
  216.6 1.2 fusion.74
  217.8 1.0 fusion.67
  218.9 1.1 multiply_bitcast_fusion
  220.8 99.6 %all-reduce.6.cloned.1.call-done = (f32[256,256]{1,0:T(8,128)}, f32[256,256]{1,0:T(8,128)}, f32[256,256]{0,1:T(8,128)}, f32[256,256]{1,0:T(8,128)}, f32[256,256]...) async-done(((f32[256,256]{1,0:T(8,128)}, f32[256,256]{1,0:T(8,128)}, ...) | async-done | bytes 2621456 | tf_op jit(solution)/shard_map/psum | solution.py:91
  320.3 1.5 convolution_add_fusion.20
  321.9 1.5 convolution_add_fusion.19
  323.4 1.5 convolution_add_fusion.14
  337.4 1.0 negate_bitcast_fusion.3
  339.9 1.3 fusion
  343.8 1.2 maximum_bitcast_fusion.2
  345.0 1.3 copy.48
  346.4 1.3 maximum_bitcast_fusion.3
  349.0 2.4 pad_maximum_fusion
  (123 shorter events, 21.0 us)
Async XLA Ops:
  7.2 109.3 %copy-start = (f32[512,512]{1,0:T(8,128)S(1)}, f32[512,512]{1,0:T(8,128)}, u32[]{:S(2)}) copy-start(f32[512,512]{1,0:T(8,128)} %param.5) | copy-start | bytes 3145732
  7.2 56.0 %all-gather.2.cloned.1.call-start = ((), (), s32[]{:S(2)}) async-start(), calls=%async_computation.4 | async-start | bytes 2621440 | tf_op jit(solution)/shard_map/all_gather | solution.py:15
  9.4 56.9 %copy-start.6 = (f32[128,256]{1,0:T(8,128)}, f32[128,256]{1,0:T(8,128)S(1)}, u32[]{:S(2)}) copy-start(f32[128,256]{1,0:T(8,128)S(1)} %convolution_multiply_fusion.3) | copy-start | bytes 393220
  10.7 55.5 %copy-start.13 = (f32[128,256]{1,0:T(8,128)}, f32[128,256]{1,0:T(8,128)S(1)}, u32[]{:S(2)}) copy-start(f32[128,256]{1,0:T(8,128)S(1)} %convolution_multiply_fusion.2) | copy-start | bytes 393220
  12.1 54.1 %copy-start.17 = (f32[128,256]{1,0:T(8,128)}, f32[128,256]{1,0:T(8,128)S(1)}, u32[]{:S(2)}) copy-start(f32[128,256]{1,0:T(8,128)S(1)} %convolution_multiply_fusion.1) | copy-start | bytes 393220
  13.5 52.8 %copy-start.19 = (f32[128,256]{1,0:T(8,128)}, f32[128,256]{1,0:T(8,128)S(1)}, u32[]{:S(2)}) copy-start(f32[128,256]{1,0:T(8,128)S(1)} %convolution_multiply_fusion) | copy-start | bytes 393220
  14.4 102.1 %all-reduce.4.cloned.1.call-start = ((), (), s32[]{:S(2)}) async-start(), calls=%async_computation.5 | async-start | bytes 4194304 | tf_op jit(solution)/shard_map/psum | solution.py:11
  66.3 74.9 %reduce-scatter.11.cloned.1.call-start = ((), (), s32[]{:S(2)}) async-start(), calls=%async_computation.9 | async-start | bytes 655360 | tf_op jit(solution)/shard_map/reduce_scatter | solution.py:80
  119.3 3.1 copy-start.1
  119.3 44.6 %reduce-scatter.9.cloned.1.call-start = ((), (), s32[]{:S(2)}) async-start(), calls=%async_computation.8 | async-start | bytes 655360 | tf_op jit(solution)/shard_map/reduce_scatter | solution.py:80
  122.3 63.7 %reduce-scatter.7.cloned.1.call-start = ((), (), s32[]{:S(2)}) async-start(), calls=%async_computation.7 | async-start | bytes 655360 | tf_op jit(solution)/shard_map/reduce_scatter | solution.py:80
  127.9 80.1 %reduce-scatter.5.cloned.1.call-start = ((), (), s32[]{:S(2)}) async-start(), calls=%async_computation.6 | async-start | bytes 655360 | tf_op jit(solution)/shard_map/reduce_scatter | solution.py:80
  137.0 183.4 %all-reduce.6.cloned.1.call-start = ((), (), s32[]{:S(2)}) async-start(), calls=%async_computation.10 | async-start | bytes 5242880 | tf_op jit(solution)/shard_map/psum | solution.py:91
  165.2 22.0 %copy-start.5 = (f32[128,256]{1,0:T(8,128)}, f32[128,256]{1,0:T(8,128)S(1)}, u32[]{:S(2)}) copy-start(f32[128,256]{1,0:T(8,128)S(1)} %convolution_add_fusion.29) | copy-start | bytes 393220
  186.0 6.7 %copy-start.14 = (f32[128,256]{1,0:T(8,128)S(1)}, f32[128,256]{1,0:T(8,128)}, u32[]{:S(2)}) copy-start(f32[128,256]{1,0:T(8,128)} %copy-done.13) | copy-start | bytes 393220
  186.0 8.8 %copy-start.7 = (f32[128,256]{1,0:T(8,128)S(1)}, f32[128,256]{1,0:T(8,128)}, u32[]{:S(2)}) copy-start(f32[128,256]{1,0:T(8,128)} %copy-done.6) | copy-start | bytes 393220
  188.5 8.4 %copy-start.16 = (f32[128,256]{1,0:T(8,128)}, f32[128,256]{1,0:T(8,128)S(1)}, u32[]{:S(2)}) copy-start(f32[128,256]{1,0:T(8,128)S(1)} %convolution_add_fusion.27) | copy-start | bytes 393220
  188.5 22.2 %copy-start.2 = (f32[128,256]{1,0:T(8,128)S(1)}, f32[128,256]{1,0:T(8,128)}, u32[]{:S(2)}) copy-start(f32[128,256]{1,0:T(8,128)} %reduce-scatter.11.cloned.1.call-done) | copy-start | bytes 393220
  208.1 5.0 %copy-start.20 = (f32[128,256]{1,0:T(8,128)S(1)}, f32[128,256]{1,0:T(8,128)}, u32[]{:S(2)}) copy-start(f32[128,256]{1,0:T(8,128)} %copy-done.19) | copy-start | bytes 393220
  208.1 6.1 %copy-start.18 = (f32[128,256]{1,0:T(8,128)S(1)}, f32[128,256]{1,0:T(8,128)}, u32[]{:S(2)}) copy-start(f32[128,256]{1,0:T(8,128)} %copy-done.17) | copy-start | bytes 393220
  208.1 7.3 %copy-start.15 = (f32[128,256]{1,0:T(8,128)S(1)}, f32[128,256]{1,0:T(8,128)}, u32[]{:S(2)}) copy-start(f32[128,256]{1,0:T(8,128)} %copy-done.13) | copy-start | bytes 393220
  208.1 8.5 %copy-start.8 = (f32[128,256]{1,0:T(8,128)S(1)}, f32[128,256]{1,0:T(8,128)}, u32[]{:S(2)}) copy-start(f32[128,256]{1,0:T(8,128)} %copy-done.6) | copy-start | bytes 393220
  211.0 5.6 %copy-start.21 = (f32[128,256]{1,0:T(8,128)}, f32[128,256]{1,0:T(8,128)S(1)}, u32[]{:S(2)}) copy-start(f32[128,256]{1,0:T(8,128)S(1)} %convolution_add_fusion.24) | copy-start | bytes 393220
  321.9 5.6 %copy-start.3 = (f32[256,256]{1,0:T(8,128)}, f32[256,256]{1,0:T(8,128)S(1)}, u32[]{:S(2)}) copy-start(f32[256,256]{1,0:T(8,128)S(1)} %convolution_add_fusion.20) | copy-start | bytes 786436
  321.9 4.5 %copy-start.36 = (f32[256,256]{1,0:T(8,128)S(1)}, f32[256,256]{1,0:T(8,128)}, u32[]{:S(2)}) copy-start(f32[256,256]{1,0:T(8,128)} %get-tuple-element.5) | copy-start | bytes 786436
  325.6 2.3 copy-start.32
  326.4 2.0 copy-start.9
  327.1 2.1 copy-start.35
  327.9 2.5 copy-start.34
  329.1 2.7 copy-start.11
  329.7 2.7 copy-start.31
  331.8 2.5 copy-start.33
  333.6 1.8 copy-start.30
  338.4 3.7 %copy-start.22 = (f32[1,256,256]{1,2,0:T(8,128)S(1)}, f32[1,256,256]{1,2,0:T(8,128)}, u32[]{:S(2)}) copy-start(f32[1,256,256]{1,2,0:T(8,128)} %get-tuple-element.21) | copy-start | bytes 786436
  339.0 4.8 %copy-start.12 = (f32[256,256]{0,1:T(8,128)S(1)}, f32[256,256]{0,1:T(8,128)}, u32[]{:S(2)}) copy-start(f32[256,256]{0,1:T(8,128)} %copy-done.11) | copy-start | bytes 786436
  343.8 2.6 copy-start.4
  345.0 2.7 copy-start.25
  346.3 1.4 copy-start.26
  346.4 1.4 copy-start.28
  346.4 1.4 copy-start.29
  346.4 1.5 copy-start.23
  346.4 1.5 copy-start.24
  346.4 1.6 copy-start.27
  347.7 1.3 copy-start.10
Sparse Core Ops, SparseCore 0:
  14.5 48.6 all-gather.1
  66.4 49.9 all-reduce.3
  119.4 21.7 reduce-scatter.10
  144.0 19.8 reduce-scatter.8
  166.1 19.8 reduce-scatter.6
  188.2 19.8 reduce-scatter.4
  217.9 102.3 all-reduce.5
where the time goes:
time: 359 us; the launch traced here: 358 us
  waiting for transfers between devices  256 us (71%)
  matrix products  65.6 us (18%)
  other arithmetic  16.4 us (5%)
  between operations  14.9 us (4%)
  local copies, waits for them, and re-layouts  5.02 us (1%)
    psum x1, waiting for transfers between devices, per_device(): summed[node] = list(lax.psum(tuple(partials), ('prow', 'pcol')))  99.6 us
    reduce_scatter x4, waiting for transfers between devices, per_device(): lax.psum_scatter(jnp.dot(anc_inverse, columns, precision=highest), 'pcol'...  57.4 us
    psum x1, waiting for transfers between devices, broadcast(): return lax.psum(jnp.where(mine, array, jnp.zeros_like(array)), axis)  50.1 us
    all_gather x1, waiting for transfers between devices, to_columns(): gathered = lax.all_gather(stacked, 'pcol', axis=1, tiled=True)  48.7 us
    dot_general x4, matrix products, per_device(): jnp.dot(anc_inverse, columns, precision=highest)  11.5 us
    dot_general x14, matrix products, window_algebra(): jnp.dot(blocks[other][second], upper_u[second], precision=highest)  9.39 us
    dot_general x6, matrix products, per_device(): jnp.dot(panels[other].T, lower_all[node], precision=highest)  8.88 us
    dot_general x6, matrix products, per_device(): jnp.dot(win_factor[other * (other - 1) // 2 + node], linv, precision=high...  8.71 us
  transfers between devices with their start and end apart: 7, of which 7 were waited for; matrix products, arithmetic and copies ran while one was open for 9% of the time, Pallas kernels for 0%

commit v1 on v0

--- a/solution.py
+++ b/solution.py
@@ -12,7 +12,24 @@
 
 
 def to_columns(stacked, per_column, pcol_at):
-    gathered = lax.all_gather(stacked, "pcol", axis=1, tiled=True)
+    size, mine_2, width = (lax.axis_size("pcol"), lax.axis_index("pcol"), stacked.shape[1])
+    forward = [(i, (i + 1) % size) for i in range(size)]
+    behind = [(i, (i - 1) % size) for i in range(size)]
+    result = jnp.zeros((*stacked.shape[:1], size * width, *stacked.shape[1 + 1 :]), stacked.dtype)
+    result = lax.dynamic_update_slice_in_dim(result, stacked, mine_2 * width, axis=1)
+    from_left = from_right = stacked
+    middle = size // 2
+    for lap in range(1, middle + 1):
+        from_left = lax.ppermute(from_left, "pcol", forward)
+        result = lax.dynamic_update_slice_in_dim(
+            result, from_left, (mine_2 - lap) % size * width, axis=1
+        )
+        if lap < size - middle:
+            from_right = lax.ppermute(from_right, "pcol", behind)
+            result = lax.dynamic_update_slice_in_dim(
+                result, from_right, (mine_2 + lap) % size * width, axis=1
+            )
+    gathered = result
     pieces = [
         broadcast(gathered, "prow", pcol_at * per_column + offset) for offset in range(per_column)
     ]

time: 359 us -> 350 us (0.975)
  waiting for transfers between devices: 256 us -> 241 us
  starting transfers between devices: 0.47 us -> 5.48 us
    all_gather x1 -> x0, waiting for transfers between devices: 48.7 us -> none  [to_columns(): gathered = lax.all_gather(stacked, 'pcol', axis=1, tiled=True)]
    ppermute x0 -> x3, waiting for transfers between devices: none -> 32.5 us  [the longest x2 23.6 us: to_columns(): from_left = lax.ppermute(from_left, 'pcol', forward)]
    ppermute x0 -> x3, starting transfers between devices: none -> 5.05 us  [the longest x2 3.02 us: to_columns(): from_left = lax.ppermute(from_left, 'pcol', forward)]
  transfers between devices with their start and end apart: 7 -> 9, of which waited for: 7 -> 9; matrix products, arithmetic and copies ran while one was open for 9% -> 10% of each run, Pallas kernels for 0% -> 0%
where the time goes in v1:
time: 350 us; the launch traced here: 349 us
  waiting for transfers between devices  241 us (69%)
  matrix products  66.2 us (19%)
  between operations  14.9 us (4%)
  other arithmetic  13.6 us (4%)
  local copies, waits for them, and re-layouts  8.01 us (2%)
  starting transfers between devices  5.48 us (2%)
    psum x1, waiting for transfers between devices, per_device(): summed[node] = list(lax.psum(tuple(partials), ('prow', 'pcol')))  99.6 us
    reduce_scatter x4, waiting for transfers between devices, per_device(): lax.psum_scatter(jnp.dot(anc_inverse, columns, precision=highest), 'pcol'...  57.5 us
    psum x1, waiting for transfers between devices, broadcast(): return lax.psum(jnp.where(mine, array, jnp.zeros_like(array)), axis)  50.8 us
    ppermute x2, waiting for transfers between devices, to_columns(): from_left = lax.ppermute(from_left, 'pcol', forward)  23.6 us
    dot_general x4, matrix products, per_device(): jnp.dot(anc_inverse, columns, precision=highest)  11.5 us
    dot_general x14, matrix products, window_algebra(): jnp.dot(blocks[other][second], upper_u[second], precision=highest)  9.38 us
    ppermute x1, waiting for transfers between devices, to_columns(): from_right = lax.ppermute(from_right, 'pcol', behind)  8.89 us
    dot_general x6, matrix products, per_device(): jnp.dot(panels[other].T, lower_all[node], precision=highest)  8.89 us
  transfers between devices with their start and end apart: 9, of which 9 were waited for; matrix products, arithmetic and copies ran while one was open for 10% of the time, Pallas kernels for 0%

profile of v1, /device:TPU:0, one launch (start us, length us, event | category | flops | bytes accessed | tf_op | source)
XLA Modules:
  0.0 348.7 jit_solution(6077640381998491846)
XLA Ops:
  8.1 1.3 convolution_multiply_fusion.3
  9.4 1.3 convolution_multiply_fusion.2
  10.8 1.3 convolution_multiply_fusion.1
  12.1 2.0 convolution_multiply_fusion
  15.9 3.0 collective-permute-start
  18.9 2.0 collective-permute-start.1
  21.0 13.1 %collective-permute-done = f32[4,128,256]{2,1,0:T(8,128)} collective-permute-done((f32[4,128,256]{2,1,0:T(8,128)}, f32[4,128,256]{2,1,0:T(8,128)}, u32[]{:S(2)}, u32[]{:S(2)}) %collective-permute-start) | collective-permute-done | bytes 524320 | tf_op jit(solution)/shard_map/ppermute | solution.py:23
  34.1 1.1 constant_dynamic-update-slice_fusion.1
  35.2 8.9 %collective-permute-done.1 = f32[4,128,256]{2,1,0:T(8,128)} collective-permute-done((f32[4,128,256]{2,1,0:T(8,128)}, f32[4,128,256]{2,1,0:T(8,128)}, u32[]{:S(2)}, u32[]{:S(2)}) %collective-permute-start.1) | collective-permute-done | bytes 524320 | tf_op jit(solution)/shard_map/ppermute | solution.py:28
  45.2 10.5 %collective-permute-done.2 = f32[4,128,256]{2,1,0:T(8,128)} collective-permute-done((f32[4,128,256]{2,1,0:T(8,128)}, f32[4,128,256]{2,1,0:T(8,128)}, u32[]{:S(2)}, u32[]{:S(2)}) %collective-permute-start.2) | collective-permute-done | bytes 524320 | tf_op jit(solution)/shard_map/ppermute | solution.py:23
  56.8 1.5 broadcast_select_fusion
  58.4 50.8 %all-reduce.4.cloned.1.call-done = f32[4,512,256]{2,1,0:T(8,128)} async-done(((f32[4,512,256]{2,1,0:T(8,128)}), f32[4,512,256]{2,1,0:T(8,128)}) %all-reduce.4.cloned.1.call-update) | async-done | bytes 2097168 | tf_op jit(solution)/shard_map/psum | solution.py:11
  109.2 2.8 convolution_bitcast_fusion
  112.1 2.9 convolution_bitcast_fusion.1
  115.2 1.3 fusion.5
  116.5 1.3 fusion.1
  117.8 2.9 convolution_bitcast_fusion.2
  120.8 1.3 fusion.3
  122.1 1.3 fusion.7
  123.5 1.3 fusion.9
  124.8 2.0 fusion.11
  126.8 2.9 convolution_bitcast_fusion.3
  130.0 4.0 %reduce-scatter.11.cloned.1.call-done = f32[128,256]{1,0:T(8,128)} async-done(((f32[512,256]{1,0:T(8,128)}), f32[128,256]{1,0:T(8,128)}) %reduce-scatter.11.cloned.1.call-update) | async-done | bytes 131088 | tf_op jit(solution)/shard_map/reduce_scatter | solution.py:97
  134.0 22.8 %reduce-scatter.9.cloned.1.call-done = f32[128,256]{1,0:T(8,128)} async-done(((f32[512,256]{1,0:T(8,128)}), f32[128,256]{1,0:T(8,128)}) %reduce-scatter.9.cloned.1.call-update) | async-done | bytes 131088 | tf_op jit(solution)/shard_map/reduce_scatter | solution.py:97
  156.7 1.4 convolution_add_fusion.29
  158.1 20.8 %reduce-scatter.7.cloned.1.call-done = f32[128,256]{1,0:T(8,128)} async-done(((f32[512,256]{1,0:T(8,128)}), f32[128,256]{1,0:T(8,128)}) %reduce-scatter.7.cloned.1.call-update) | async-done | bytes 131088 | tf_op jit(solution)/shard_map/reduce_scatter | solution.py:97
  178.9 1.3 convolution_add_fusion.28
  180.1 1.2 convolution_add_fusion.27
  181.4 2.2 fusion.80
  183.6 2.0 fusion.79
  185.6 2.1 fusion.66
  187.7 2.1 fusion.65
  189.7 1.2 fusion.63
  190.9 9.9 %reduce-scatter.5.cloned.1.call-done = f32[128,256]{1,0:T(8,128)} async-done(((f32[512,256]{1,0:T(8,128)}), f32[128,256]{1,0:T(8,128)}) %reduce-scatter.5.cloned.1.call-update) | async-done | bytes 131088 | tf_op jit(solution)/shard_map/reduce_scatter | solution.py:97
  200.9 1.3 convolution_add_fusion.26
  202.2 1.2 convolution_add_fusion.25
  203.8 2.1 fusion.78
  205.9 1.1 fusion.81
  207.0 1.2 fusion.76
  208.2 1.2 fusion.75
  209.4 1.2 fusion.74
  213.6 99.6 %all-reduce.6.cloned.1.call-done = (f32[256,256]{1,0:T(8,128)}, f32[256,256]{1,0:T(8,128)}, f32[256,256]{0,1:T(8,128)}, f32[256,256]{1,0:T(8,128)}, f32[256,256]...) async-done(((f32[256,256]{1,0:T(8,128)}, f32[256,256]{1,0:T(8,128)}, ...) | async-done | bytes 2621456 | tf_op jit(solution)/shard_map/psum | solution.py:108
  313.2 1.5 convolution_add_fusion.20
  314.8 1.5 convolution_add_fusion.19
  316.3 1.5 convolution_add_fusion.14
  333.0 1.3 fusion
  337.8 1.3 maximum_bitcast_fusion.3
  339.4 2.4 pad_maximum_fusion
  (132 shorter events, 27.1 us)
Async XLA Ops:
  7.2 102.1 %copy-start = (f32[512,512]{1,0:T(8,128)S(1)}, f32[512,512]{1,0:T(8,128)}, u32[]{:S(2)}) copy-start(f32[512,512]{1,0:T(8,128)} %param.5) | copy-start | bytes 3145732
  7.2 102.0 %all-reduce.4.cloned.1.call-start = ((), (), s32[]{:S(2)}) async-start(), calls=%async_computation.4 | async-start | bytes 4194304 | tf_op jit(solution)/shard_map/psum | solution.py:11
  9.4 48.9 %copy-start.6 = (f32[128,256]{1,0:T(8,128)}, f32[128,256]{1,0:T(8,128)S(1)}, u32[]{:S(2)}) copy-start(f32[128,256]{1,0:T(8,128)S(1)} %convolution_multiply_fusion.3) | copy-start | bytes 393220
  10.7 47.6 %copy-start.12 = (f32[128,256]{1,0:T(8,128)}, f32[128,256]{1,0:T(8,128)S(1)}, u32[]{:S(2)}) copy-start(f32[128,256]{1,0:T(8,128)S(1)} %convolution_multiply_fusion.2) | copy-start | bytes 393220
  12.1 3.8 %copy-start.18 = (f32[128,256]{1,0:T(8,128)}, f32[128,256]{1,0:T(8,128)S(1)}, u32[]{:S(2)}) copy-start(f32[128,256]{1,0:T(8,128)S(1)} %convolution_multiply_fusion.1) | copy-start | bytes 393220
  14.1 0.9 copy-start.20
  15.9 18.2 %collective-permute-start = (f32[4,128,256]{2,1,0:T(8,128)}, f32[4,128,256]{2,1,0:T(8,128)}, u32[]{:S(2)}, u32[]{:S(2)}) collective-permute-start(f32[4,128,256]{2,1,0:T(8,128)} %get-tuple-element.12), channel_id=1, source_target_pairs={{0,1},{1,2},{2,3},{3,0},{4,5},{5,6},{6,7},{7,4},{8,9},{9,10},{10,1... | collective-permute-start | bytes 1572872 | tf_op jit(solution)/shard_map/ppermute | solution.py:23
  18.9 25.2 %collective-permute-start.1 = (f32[4,128,256]{2,1,0:T(8,128)}, f32[4,128,256]{2,1,0:T(8,128)}, u32[]{:S(2)}, u32[]{:S(2)}) collective-permute-start(f32[4,128,256]{2,1,0:T(8,128)} %get-tuple-element.12), channel_id=1, source_target_pairs={{0,3},{1,0},{2,1},{3,2},{4,7},{5,4},{6,5},{7,6},{8,11},{9,8},{10,9... | collective-permute-start | bytes 1572872 | tf_op jit(solution)/shard_map/ppermute | solution.py:28
  34.1 21.6 %collective-permute-start.2 = (f32[4,128,256]{2,1,0:T(8,128)}, f32[4,128,256]{2,1,0:T(8,128)}, u32[]{:S(2)}, u32[]{:S(2)}) collective-permute-start(f32[4,128,256]{2,1,0:T(8,128)} %collective-permute-done), channel_id=1, source_target_pairs={{0,1},{1,2},{2,3},{3,0},{4,5},{5,6},{6,7},{7,4},{8,9},{9,10},{10,1... | collective-permute-start | bytes 1572872 | tf_op jit(solution)/shard_map/ppermute | solution.py:23
  58.4 75.6 %reduce-scatter.11.cloned.1.call-start = ((), (), s32[]{:S(2)}) async-start(), calls=%async_computation.8 | async-start | bytes 655360 | tf_op jit(solution)/shard_map/reduce_scatter | solution.py:97
  112.1 3.1 copy-start.1
  112.1 44.6 %reduce-scatter.9.cloned.1.call-start = ((), (), s32[]{:S(2)}) async-start(), calls=%async_computation.7 | async-start | bytes 655360 | tf_op jit(solution)/shard_map/reduce_scatter | solution.py:97
  115.1 63.8 %reduce-scatter.7.cloned.1.call-start = ((), (), s32[]{:S(2)}) async-start(), calls=%async_computation.6 | async-start | bytes 655360 | tf_op jit(solution)/shard_map/reduce_scatter | solution.py:97
  120.7 80.2 %reduce-scatter.5.cloned.1.call-start = ((), (), s32[]{:S(2)}) async-start(), calls=%async_computation.5 | async-start | bytes 655360 | tf_op jit(solution)/shard_map/reduce_scatter | solution.py:97
  129.7 183.5 %all-reduce.6.cloned.1.call-start = ((), (), s32[]{:S(2)}) async-start(), calls=%async_computation.9 | async-start | bytes 5242880 | tf_op jit(solution)/shard_map/psum | solution.py:108
  158.1 22.0 %copy-start.5 = (f32[128,256]{1,0:T(8,128)}, f32[128,256]{1,0:T(8,128)S(1)}, u32[]{:S(2)}) copy-start(f32[128,256]{1,0:T(8,128)S(1)} %convolution_add_fusion.29) | copy-start | bytes 393220
  178.9 6.7 %copy-start.13 = (f32[128,256]{1,0:T(8,128)S(1)}, f32[128,256]{1,0:T(8,128)}, u32[]{:S(2)}) copy-start(f32[128,256]{1,0:T(8,128)} %copy-done.12) | copy-start | bytes 393220
  178.9 8.8 %copy-start.7 = (f32[128,256]{1,0:T(8,128)S(1)}, f32[128,256]{1,0:T(8,128)}, u32[]{:S(2)}) copy-start(f32[128,256]{1,0:T(8,128)} %copy-done.6) | copy-start | bytes 393220
  181.4 8.4 %copy-start.15 = (f32[128,256]{1,0:T(8,128)}, f32[128,256]{1,0:T(8,128)S(1)}, u32[]{:S(2)}) copy-start(f32[128,256]{1,0:T(8,128)S(1)} %convolution_add_fusion.27) | copy-start | bytes 393220
  181.4 22.1 %copy-start.2 = (f32[128,256]{1,0:T(8,128)S(1)}, f32[128,256]{1,0:T(8,128)}, u32[]{:S(2)}) copy-start(f32[128,256]{1,0:T(8,128)} %reduce-scatter.11.cloned.1.call-done) | copy-start | bytes 393220
  200.9 5.0 %copy-start.21 = (f32[128,256]{1,0:T(8,128)S(1)}, f32[128,256]{1,0:T(8,128)}, u32[]{:S(2)}) copy-start(f32[128,256]{1,0:T(8,128)} %convolution_multiply_fusion) | copy-start | bytes 393220
  200.9 6.1 %copy-start.19 = (f32[128,256]{1,0:T(8,128)S(1)}, f32[128,256]{1,0:T(8,128)}, u32[]{:S(2)}) copy-start(f32[128,256]{1,0:T(8,128)} %copy-done.18) | copy-start | bytes 393220
  200.9 7.3 %copy-start.14 = (f32[128,256]{1,0:T(8,128)S(1)}, f32[128,256]{1,0:T(8,128)}, u32[]{:S(2)}) copy-start(f32[128,256]{1,0:T(8,128)} %copy-done.12) | copy-start | bytes 393220
  200.9 8.5 %copy-start.8 = (f32[128,256]{1,0:T(8,128)S(1)}, f32[128,256]{1,0:T(8,128)}, u32[]{:S(2)}) copy-start(f32[128,256]{1,0:T(8,128)} %copy-done.6) | copy-start | bytes 393220
  203.8 5.6 %copy-start.22 = (f32[128,256]{1,0:T(8,128)}, f32[128,256]{1,0:T(8,128)S(1)}, u32[]{:S(2)}) copy-start(f32[128,256]{1,0:T(8,128)S(1)} %convolution_add_fusion.24) | copy-start | bytes 393220
  314.7 5.6 %copy-start.3 = (f32[256,256]{1,0:T(8,128)}, f32[256,256]{1,0:T(8,128)S(1)}, u32[]{:S(2)}) copy-start(f32[256,256]{1,0:T(8,128)S(1)} %convolution_add_fusion.20) | copy-start | bytes 786436
  314.8 4.6 %copy-start.37 = (f32[256,256]{1,0:T(8,128)S(1)}, f32[256,256]{1,0:T(8,128)}, u32[]{:S(2)}) copy-start(f32[256,256]{1,0:T(8,128)} %get-tuple-element.5) | copy-start | bytes 786436
  318.5 2.3 copy-start.33
  319.3 2.0 copy-start.9
  319.9 2.1 copy-start.36
  320.7 2.5 copy-start.35
  322.0 2.7 copy-start.10
  322.6 2.7 copy-start.32
  324.6 2.5 copy-start.34
  326.5 2.1 copy-start.31
  327.1 0.7 copy-start.16
  331.5 3.7 %copy-start.23 = (f32[1,256,256]{1,2,0:T(8,128)S(1)}, f32[1,256,256]{1,2,0:T(8,128)}, u32[]{:S(2)}) copy-start(f32[1,256,256]{1,2,0:T(8,128)} %get-tuple-element.23) | copy-start | bytes 786436
  332.1 4.8 %copy-start.11 = (f32[256,256]{0,1:T(8,128)S(1)}, f32[256,256]{0,1:T(8,128)}, u32[]{:S(2)}) copy-start(f32[256,256]{0,1:T(8,128)} %copy-done.10) | copy-start | bytes 786436
  336.8 1.0 copy-start.4
  337.3 1.8 copy-start.26
  337.3 1.8 copy-start.27
  337.3 1.8 copy-start.29
  337.3 1.8 copy-start.30
  337.8 1.4 copy-start.17
  337.8 1.4 copy-start.24
  337.8 1.4 copy-start.25
  337.8 1.5 copy-start.28
Sparse Core Ops, SparseCore 0:
  58.5 50.7 all-reduce.3
  112.2 21.7 reduce-scatter.10
  136.9 19.7 reduce-scatter.8
  159.0 19.8 reduce-scatter.6
  181.1 19.7 reduce-scatter.4
  210.7 102.4 all-reduce.5
